TPU v7x, 512 devices: a whole 4x4x16 slice. The times are simulated.
512 devices in a mesh: grp: 16 (over y_hi, x, core), seq: 32 (over z, y_lo).
Axes of the slice: x: 4, y: 4 (y_hi: 2, y_lo: 2; y = y_hi * 2 + y_lo), z: 16, core: 2. Of those that a mesh axis runs over, the one named last changes fastest.
Arguments:
- tokens: bfloat16 [32, 64, 128, 512], P(None, 'grp', 'seq'), may hold values from -6 to 6
- cotangent: bfloat16 [32, 64, 128, 512], P(None, 'grp', 'seq'), may hold values from -6 to 6
- gate_weight: bfloat16 [512, 512], replicated, may hold values from -0.25 to 0.25
- first_factor: bfloat16 [4, 32, 32], replicated, may hold values from -1 to 1
- middle_factor: bfloat16 [4, 64, 64], replicated, may hold values from -0.75 to 0.75
- last_factor: bfloat16 [4, 128, 128], replicated, may hold values from -0.5 to 0.5
Outputs:
- d_tokens: bfloat16 [32, 64, 128, 512], P(None, 'grp', 'seq')
- grad_gate: float32 [512, 512], P('seq')
- grad_first: float32 [4, 32, 32], replicated
- grad_middle: float32 [4, 64, 64], P(None, 'grp')
- grad_last: float32 [4, 128, 128], P(None, 'seq')
All inputs are finite; a program needn't handle non-finite values.
Results may differ from a plain program's by a relative error of at most 0.0065.
Values may be sent and summed in bfloat16 or wider, within the bound.
A program may use at most 64 MiB of HBM per device.

v0:
```python
import math

import jax
import jax.numpy as jnp
from jax import lax
from jax.sharding import PartitionSpec as P

HEADS = 4


def split_up(shard, dim, length):
    before, after = (shard.shape[:dim], shard.shape[dim + 1 :])
    return jnp.moveaxis(shard.reshape(*before, length, -1, *after), dim, 0)


def sum_together(arrays, axis, dims):
    length = lax.axis_size(axis)
    tiles = [split_up(a, dim, length) for a, dim in zip(arrays, dims)]
    lines = jnp.concatenate([b.reshape(length, -1) for b in tiles], axis=1)
    extent = max(16, -(-lines.shape[1] // 1024) * 8)
    lines = jnp.pad(lines, ((0, 0), (0, extent * 128 - lines.shape[1]))).reshape(-1, 128)
    vector, at, finished = (lax.psum_scatter(lines, axis, tiled=True).reshape(-1), 0, [])
    for b in tiles:
        part = b[0]
        finished.append(vector[at : at + part.size].reshape(part.shape))
        at += part.size
    return tuple(finished)


def sum_at_owner(shard, axis, dim):
    tiles = split_up(shard, dim, lax.axis_size(axis))
    arrived = lax.all_to_all(tiles, axis, split_axis=0, concat_axis=0, tiled=True)
    return arrived.sum(axis=0)


def copy_for_each(shard, axis):
    copies = jnp.broadcast_to(shard, (lax.axis_size(axis), *shard.shape))
    return lax.all_to_all(copies, axis, split_axis=0, concat_axis=0, tiled=True)


def over_copies(shard, axis):
    return copy_for_each(shard, axis).sum(axis=0)


def in_one(arrays, axis):
    ends = [0]
    for a in arrays:
        ends.append(ends[-1] + a.size)
    total = over_copies(jnp.concatenate([a.ravel() for a in arrays]), axis)
    return tuple((total[b:e].reshape(a.shape) for a, b, e in zip(arrays, ends, ends[1:])))


def headed(values):
    return values.reshape(values.shape[:-1] + (HEADS, values.shape[-1] // HEADS))


def mixing(weights, values, form):
    result = jnp.einsum(form, weights, headed(values), preferred_element_type=jnp.float32)
    return result.reshape(values.shape)


def contract(left, right, form):
    return jnp.einsum(form, headed(left), headed(right), preferred_element_type=jnp.float32)


def send_last(values):
    return lax.all_to_all(values, "seq", split_axis=0, concat_axis=2, tiled=True)


def send_middle(values):
    return lax.all_to_all(values, "grp", split_axis=2, concat_axis=1, tiled=True)


def return_middle(values):
    return lax.all_to_all(values, "grp", split_axis=1, concat_axis=2, tiled=True)


def return_last(values):
    return lax.all_to_all(values, "seq", split_axis=2, concat_axis=0, tiled=True)


def shards(tokens, cotangent, gate_weight, first_factor, middle_factor, last_factor):
    width = tokens.shape[-1]
    rows = tokens.reshape(-1, width)
    gate = jax.nn.sigmoid(jnp.dot(rows, gate_weight, preferred_element_type=jnp.float32)).reshape(
        tokens.shape
    )
    first_out = mixing(first_factor, tokens, "hab,bjkhe->ajkhe").astype(jnp.bfloat16)
    last_in = send_last(first_out)
    last_out = mixing(last_factor, last_in, "hab,ijbhe->ijahe").astype(jnp.bfloat16)
    middle_in = send_middle(last_out)
    middle_out = mixing(middle_factor, middle_in, "hab,ibkhe->iakhe").astype(jnp.bfloat16)
    mixer = return_last(return_middle(middle_out))
    upstream = cotangent.astype(jnp.float32)
    d_mix = (upstream * gate).astype(jnp.bfloat16)
    d_pre = (upstream * mixer.astype(jnp.float32) * gate * (1.0 - gate)).astype(jnp.bfloat16)
    pre_rows = d_pre.reshape(-1, width)
    gate_part = jnp.einsum("tc,td->cd", rows, pre_rows, preferred_element_type=jnp.float32)
    gate_term = jnp.einsum("td,cd->tc", pre_rows, gate_weight, preferred_element_type=jnp.float32)
    middle_grad_in = send_middle(send_last(d_mix))
    middle_back = mixing(middle_factor, middle_grad_in, "hba,ibkhe->iakhe").astype(jnp.bfloat16)
    middle_part = contract(middle_grad_in, middle_in, "iakhe,ibkhe->hab")
    last_back_in = return_middle(middle_back)
    last_back = mixing(last_factor, last_back_in, "hba,ijbhe->ijahe").astype(jnp.bfloat16)
    last_part = contract(last_back_in, last_in, "ijahe,ijbhe->hab")
    first_back_in = return_last(last_back)
    first_back = mixing(first_factor, first_back_in, "hba,bjkhe->ajkhe")
    first_part = contract(first_back_in, tokens, "ajkhe,bjkhe->hab")
    d_tokens = (
        (first_back.reshape(-1, width) + gate_term).astype(jnp.bfloat16).reshape(tokens.shape)
    )
    total = (
        tokens.shape[0]
        * tokens.shape[1]
        * tokens.shape[2]
        * lax.axis_size("grp")
        * lax.axis_size("seq")
    )
    factor = 1.0 / math.sqrt(total)
    gate_share, last_share = sum_together((gate_part, last_part), "seq", (0, 1))
    middle_share = sum_at_owner(middle_part, "grp", 1)
    gate_sum, last_sum, first_half = in_one((gate_share, last_share, first_part), "grp")
    middle_sum, first_sum = in_one((middle_share, first_half), "seq")
    return (d_tokens, gate_sum * factor, first_sum * factor, middle_sum * factor, last_sum * factor)


def solution(mesh):
    in_specs = (P(None, "grp", "seq", None), P(None, "grp", "seq", None), P(), P(), P(), P())
    out_specs = (
        P(None, "grp", "seq", None),
        P("seq", None),
        P(),
        P(None, "grp", None),
        P(None, "seq", None),
    )
    return jax.shard_map(shards, mesh=mesh, in_specs=in_specs, out_specs=out_specs, check_vma=False)
```

profile of v0, /device:TPU:1, one launch (start us, length us, event | category | flops | bytes accessed | tf_op | source)
XLA Modules:
  0.0 427.2 jit_solution(16249440475941955132)
XLA Ops:
  7.2 1.3 reshape.215
  8.5 1.6 fusion.5
  10.7 48.2 %all_to_all.137 = bf16[32,4,4,512]{3,2,1,0:T(4,128)(2,1)S(1)} all-to-all(bf16[32,4,4,512]{3,2,1,0:T(4,128)(2,1)S(1)} %reshape.238), channel_id=1, replica_groups=mesh['grp'=16,'seq'=32] {'seq'}, dimensions={0} | all-to-all | bytes 1048576 | tf_op jit(solution)/shard_map/all_to_all | solution.py:67
  60.6 20.0 %all_to_all.138 = bf16[1,4,128,512]{3,1,0,2:T(4,128)(2,1)S(1)} all-to-all(bf16[1,4,128,512]{3,1,0,2:T(4,128)(2,1)S(1)} %copy.389), channel_id=1, replica_groups=mesh['grp'=16,'seq'=32] {'grp'}, dimensions={2} | all-to-all | bytes 1048576 | tf_op jit(solution)/shard_map/all_to_all | solution.py:71
  80.8 0.7 copy-done.14
  82.2 15.0 %all_to_all.139 = bf16[1,64,8,512]{3,2,0,1:T(8,128)(2,1)S(1)} all-to-all(bf16[1,64,8,512]{3,2,0,1:T(8,128)(2,1)S(1)} %bitcast.151), channel_id=1, replica_groups=mesh['grp'=16,'seq'=32] {'grp'}, dimensions={1} | all-to-all | bytes 1048576 | tf_op jit(solution)/shard_map/all_to_all | solution.py:75
  97.2 1.2 copy.396
  98.4 3.9 all-to-all-start.7
  102.5 1.5 fusion.2
  104.0 1.5 reshape.211
  105.5 27.3 %all-to-all-done.7 = bf16[1,4,128,512]{3,1,0,2:T(4,128)(2,1)S(1)} async-done(((bf16[1,4,128,512]{3,1,0,2:T(4,128)(2,1)}), bf16[1,4,128,512]{3,1,0,2:T(4,128)(2,1)S(1)}, u32[]{:S(2)}, u32[]{:S(2)}) %all-to-all-start.7) | async-done | bytes 524320 | tf_op jit(solution)/shard_map/all_to_all | solution.py:79
  133.0 1.5 fusion.9
  135.0 35.6 %all_to_all.140 = bf16[32,4,4,512]{3,2,1,0:T(4,128)(2,1)S(1)} all-to-all(bf16[32,4,4,512]{3,2,1,0:T(4,128)(2,1)S(1)} %copy.366), channel_id=1, replica_groups=mesh['grp'=16,'seq'=32] {'seq'}, dimensions={0} | all-to-all | bytes 1048576 | tf_op jit(solution)/shard_map/all_to_all | solution.py:67
  170.8 18.3 %all_to_all.141 = bf16[1,4,128,512]{3,1,0,2:T(4,128)(2,1)S(1)} all-to-all(bf16[1,4,128,512]{3,1,0,2:T(4,128)(2,1)S(1)} %bitcast.155), channel_id=1, replica_groups=mesh['grp'=16,'seq'=32] {'grp'}, dimensions={2} | all-to-all | bytes 1048576 | tf_op jit(solution)/shard_map/all_to_all | solution.py:71
  189.7 1.1 copy.483
  190.8 5.4 %all-to-all-start.2 = ((bf16[1,64,8,512]{3,2,0,1:T(8,128)(2,1)}), bf16[1,64,8,512]{3,2,0,1:T(8,128)(2,1)}, u32[]{:S(2)}, u32[]{:S(2)}) async-start(bf16[1,64,8,512]{3,2,0,1:T(8,128)(2,1)} %bitcast.137), calls=%async_computation.2 | async-start | bytes 1048576 | tf_op jit(solution)/shard_map/all_to_all | solution.py:75
  196.4 1.6 convolution_bitcast_fusion.1
  198.0 1.6 copy.402
  199.8 7.6 %all-to-all-done.2 = bf16[1,64,8,512]{3,2,0,1:T(8,128)(2,1)} async-done(((bf16[1,64,8,512]{3,2,0,1:T(8,128)(2,1)}), bf16[1,64,8,512]{3,2,0,1:T(8,128)(2,1)}, u32[]{:S(2)}, u32[]{:S(2)}) %all-to-all-start.2) | async-done | bytes 524320 | tf_op jit(solution)/shard_map/all_to_all | solution.py:75
  207.4 1.9 copy.482
  209.3 1.2 reshape.213
  211.3 0.8 reshape.221
  212.1 1.0 pad_maximum_fusion
  213.1 1.3 reshape.222
  214.4 1.0 copy-done.11
  215.8 1.2 copy.378
  217.0 3.9 all-to-all-start.3
  221.4 0.8 reshape.239
  222.1 29.3 %all-to-all-done.3 = bf16[1,4,128,512]{3,1,0,2:T(4,128)(2,1)S(1)} async-done(((bf16[1,4,128,512]{3,1,0,2:T(4,128)(2,1)}), bf16[1,4,128,512]{3,1,0,2:T(4,128)(2,1)S(1)}, u32[]{:S(2)}, u32[]{:S(2)}) %all-to-all-start.3) | async-done | bytes 524320 | tf_op jit(solution)/shard_map/all_to_all | solution.py:79
  251.5 6.7 %all-to-all-start.9 = ((f32[16,1,1024]{2,1,0:T(1,128)}), f32[16,1,1024]{2,1,0:T(1,128)S(1)}, u32[]{:S(2)}, u32[]{:S(2)}) async-start(f32[16,1,1024]{2,1,0:T(1,128)} %reshape.239), calls=%async_computation.10 | async-start | bytes 131072 | tf_op jit(solution)/shard_map/all_to_all | solution.py:32
  258.4 0.7 convolution_bitcast_fusion.2
  259.2 63.6 %reduce-scatter.2.cloned.1.call-done = f32[80,128]{1,0:T(8,128)} async-done(((f32[2560,128]{1,0:T(8,128)}), f32[80,128]{1,0:T(8,128)}) %reduce-scatter.2.cloned.1.call-update) | async-done | bytes 40976 | tf_op jit(solution)/shard_map/reduce_scatter | solution.py:22
  322.7 0.7 slice_bitcast_fusion.1
  323.4 0.8 slice_bitcast_fusion
  324.2 1.4 broadcast_in_dim.6
  325.6 30.7 %all-to-all-start.8 = ((f32[16,1,14336]{2,1,0:T(1,128)}), f32[16,1,14336]{2,1,0:T(1,128)S(1)}, u32[]{:S(2)}, u32[]{:S(2)}) async-start(f32[16,1,14336]{2,1,0:T(1,128)} %broadcast_in_dim.6), calls=%async_computation.9 | async-start | bytes 1835008 | tf_op jit(solution)/shard_map/all_to_all | solution.py:38
  356.8 0.8 reduce.2
  357.9 14.3 %all-to-all-done.8 = f32[16,1,14336]{2,1,0:T(1,128)S(1)} async-done(((f32[16,1,14336]{2,1,0:T(1,128)}), f32[16,1,14336]{2,1,0:T(1,128)S(1)}, u32[]{:S(2)}, u32[]{:S(2)}) %all-to-all-start.8) | async-done | bytes 917536 | tf_op jit(solution)/shard_map/all_to_all | solution.py:38
  372.7 1.2 broadcast_in_dim.7
  373.9 8.1 %all-to-all-start.10 = ((f32[32,1,5120]{2,1,0:T(1,128)}), f32[32,1,5120]{2,1,0:T(1,128)S(1)}, u32[]{:S(2)}, u32[]{:S(2)}) async-start(f32[32,1,5120]{2,1,0:T(1,128)} %broadcast_in_dim.7), calls=%async_computation.11 | async-start | bytes 1310720 | tf_op jit(solution)/shard_map/all_to_all | solution.py:38
  382.8 0.8 convolution_bitcast_fusion
  383.6 0.7 copy.382
  384.7 0.9 reshape.219
  385.6 0.6 mul.54
  386.3 0.6 slice_multiply_fusion.2
  386.9 31.7 %all-to-all-done.10 = f32[32,1,5120]{2,1,0:T(1,128)S(1)} async-done(((f32[32,1,5120]{2,1,0:T(1,128)}), f32[32,1,5120]{2,1,0:T(1,128)S(1)}, u32[]{:S(2)}, u32[]{:S(2)}) %all-to-all-start.10) | async-done | bytes 655392 | tf_op jit(solution)/shard_map/all_to_all | solution.py:38
  419.0 0.7 mul.60
  419.6 0.7 mul.57
  (76 shorter events, 9.8 us)
Async XLA Ops:
  7.2 95.3 %copy-start = (bf16[512,512]{1,0:T(8,128)(2,1)S(1)}, bf16[512,512]{1,0:T(8,128)(2,1)}, u32[]{:S(2)}) copy-start(bf16[512,512]{1,0:T(8,128)(2,1)} %param.8) | copy-start | bytes 1572868
  8.5 2.2 copy-start.2
  58.9 0.9 copy-start.13
  59.8 0.8 copy-start.6
  80.7 0.8 copy-start.14
  80.8 16.3 %copy-start.4 = (bf16[1,16,4,8,512]{4,3,2,1,0:T(8,128)(2,1)}, bf16[1,16,4,8,512]{4,3,2,1,0:T(8,128)(2,1)S(1)}, u32[]{:S(2)}) copy-start(bf16[1,16,4,8,512]{4,3,2,1,0:T(8,128)(2,1)S(1)} %copy.391) | copy-start | bytes 1572868
  97.2 5.1 %copy-start.1 = (bf16[32,4,4,512]{3,2,1,0:T(4,128)(2,1)S(1)}, bf16[32,4,4,512]{3,2,1,0:T(4,128)(2,1)}, u32[]{:S(2)}) copy-start(bf16[32,4,4,512]{3,2,1,0:T(4,128)(2,1)} %param.6) | copy-start | bytes 1572868
  98.4 34.5 %all-to-all-start.7 = ((bf16[1,4,128,512]{3,1,0,2:T(4,128)(2,1)}), bf16[1,4,128,512]{3,1,0,2:T(4,128)(2,1)S(1)}, u32[]{:S(2)}, u32[]{:S(2)}) async-start(bf16[1,4,128,512]{3,1,0,2:T(4,128)(2,1)} %copy.396), calls=%async_computation.7 | async-start | bytes 1048576 | tf_op jit(solution)/shard_map/all_to_all | solution.py:79
  105.5 27.5 %copy-start.12 = (bf16[32,4,4,512]{3,2,1,0:T(4,128)(2,1)S(1)}, bf16[32,4,4,512]{3,2,1,0:T(4,128)(2,1)}, u32[]{:S(2)}) copy-start(bf16[32,4,4,512]{3,2,1,0:T(4,128)(2,1)} %param.7) | copy-start | bytes 1572868
  189.3 1.5 copy-start.8
  190.8 16.6 %all-to-all-start.2 = ((bf16[1,64,8,512]{3,2,0,1:T(8,128)(2,1)}), bf16[1,64,8,512]{3,2,0,1:T(8,128)(2,1)}, u32[]{:S(2)}, u32[]{:S(2)}) async-start(bf16[1,64,8,512]{3,2,0,1:T(8,128)(2,1)} %bitcast.137), calls=%async_computation.2 | async-start | bytes 1048576 | tf_op jit(solution)/shard_map/all_to_all | solution.py:75
  196.2 126.5 %reduce-scatter.2.cloned.1.call-start = ((), (), s32[]{:S(2)}) async-start(), calls=%async_computation.12 | async-start | bytes 1351680 | tf_op jit(solution)/shard_map/reduce_scatter | solution.py:22
  199.8 10.7 %copy-start.7 = (bf16[4,128,4,128]{3,2,1,0:T(4,128)(2,1)S(1)}, bf16[4,128,4,128]{3,2,1,0:T(4,128)(2,1)}, u32[]{:S(2)}) copy-start(bf16[4,128,4,128]{3,2,1,0:T(4,128)(2,1)} %copy-done.6) | copy-start | bytes 1572868
  210.5 0.8 copy-start.10
  214.4 1.0 copy-start.11
  215.8 5.1 %copy-start.5 = (bf16[1,16,4,8,512]{4,3,2,1,0:T(8,128)(2,1)S(1)}, bf16[1,16,4,8,512]{4,3,2,1,0:T(8,128)(2,1)}, u32[]{:S(2)}) copy-start(bf16[1,16,4,8,512]{4,3,2,1,0:T(8,128)(2,1)} %copy-done.4) | copy-start | bytes 1572868
  215.8 5.1 %copy-start.9 = (bf16[1,16,4,8,512]{4,3,2,1,0:T(8,128)(2,1)S(1)}, bf16[1,16,4,8,512]{4,3,2,1,0:T(8,128)(2,1)}, u32[]{:S(2)}) copy-start(bf16[1,16,4,8,512]{4,3,2,1,0:T(8,128)(2,1)} %copy-done.8) | copy-start | bytes 1572868
  217.0 34.5 %all-to-all-start.3 = ((bf16[1,4,128,512]{3,1,0,2:T(4,128)(2,1)}), bf16[1,4,128,512]{3,1,0,2:T(4,128)(2,1)S(1)}, u32[]{:S(2)}, u32[]{:S(2)}) async-start(bf16[1,4,128,512]{3,1,0,2:T(4,128)(2,1)} %copy.378), calls=%async_computation.3 | async-start | bytes 1048576 | tf_op jit(solution)/shard_map/all_to_all | solution.py:79
  220.9 37.5 %copy-start.3 = (bf16[32,4,4,4,128]{4,3,2,1,0:T(4,128)(2,1)S(1)}, bf16[32,4,4,4,128]{4,3,2,1,0:T(4,128)(2,1)}, u32[]{:S(2)}) copy-start(bf16[32,4,4,4,128]{4,3,2,1,0:T(4,128)(2,1)} %copy-done.2) | copy-start | bytes 1572868
  251.5 72.7 %all-to-all-start.9 = ((f32[16,1,1024]{2,1,0:T(1,128)}), f32[16,1,1024]{2,1,0:T(1,128)S(1)}, u32[]{:S(2)}, u32[]{:S(2)}) async-start(f32[16,1,1024]{2,1,0:T(1,128)} %reshape.239), calls=%async_computation.10 | async-start | bytes 131072 | tf_op jit(solution)/shard_map/all_to_all | solution.py:32
  325.6 46.5 %all-to-all-start.8 = ((f32[16,1,14336]{2,1,0:T(1,128)}), f32[16,1,14336]{2,1,0:T(1,128)S(1)}, u32[]{:S(2)}, u32[]{:S(2)}) async-start(f32[16,1,14336]{2,1,0:T(1,128)} %broadcast_in_dim.6), calls=%async_computation.9 | async-start | bytes 1835008 | tf_op jit(solution)/shard_map/all_to_all | solution.py:38
  373.9 44.7 %all-to-all-start.10 = ((f32[32,1,5120]{2,1,0:T(1,128)}), f32[32,1,5120]{2,1,0:T(1,128)S(1)}, u32[]{:S(2)}, u32[]{:S(2)}) async-start(f32[32,1,5120]{2,1,0:T(1,128)} %broadcast_in_dim.7), calls=%async_computation.11 | async-start | bytes 1310720 | tf_op jit(solution)/shard_map/all_to_all | solution.py:38
  382.0 0.8 copy-start.15
Sparse Core Ops, SparseCore 0:
  214.5 108.1 reduce-scatter.1
where the time goes:
time: 430 us; the launch traced here: 427 us
  waiting for transfers between devices  174 us (40%)
  blocking collectives  137 us (32%)
  starting transfers between devices  58.9 us (14%)
  local copies, waits for them, and re-layouts  29 us (7%)
  between operations  14.5 us (3%)
  matrix products  8.62 us (2%)
  other arithmetic  5.13 us (1%)
    all_to_all x2, blocking collectives, send_last(): lax.all_to_all(values, 'seq', split_axis=0, concat_axis=2, tiled=True)  83.8 us
    reduce_scatter x1, waiting for transfers between devices, sum_together(): lax.psum_scatter(lines, axis, tiled=True).reshape(-1)  63.6 us
    all_to_all x2, waiting for transfers between devices, return_last(): lax.all_to_all(values, 'seq', split_axis=2, concat_axis=0, tiled=True)  56.7 us
    all_to_all x2, waiting for transfers between devices, copy_for_each(): return lax.all_to_all(copies, axis, split_axis=0, concat_axis=0, tiled=True)  45.9 us
    all_to_all x2, starting transfers between devices, copy_for_each(): return lax.all_to_all(copies, axis, split_axis=0, concat_axis=0, tiled=True)  38.8 us
    all_to_all x2, blocking collectives, send_middle(): lax.all_to_all(values, 'grp', split_axis=2, concat_axis=1, tiled=True)  38.3 us
    all_to_all x1, blocking collectives, return_middle(): lax.all_to_all(values, 'grp', split_axis=1, concat_axis=2, tiled=True)  15 us
  transfers between devices with their start and end apart: 7, of which 6 were waited for; matrix products, arithmetic and copies ran while one was open for 4% of the time, Pallas kernels for 0%

commit v1 on v0

v1 whole, which is shorter than its diff:
```python
import jax
import jax.numpy as jnp
from jax import lax
from jax.experimental import pallas as pl
from jax.experimental.pallas import tpu as pltpu
from jax.sharding import PartitionSpec as P

MESH = pl.DeviceIdType.MESH
BF = jnp.bfloat16
F32 = jnp.float32
SCALE = 1.0 / 512.0
HIGH = lax.Precision.HIGHEST


def mm(a, b):
    return jnp.dot(a, b, preferred_element_type=F32)


def tn(a, b):
    return lax.dot_general(a, b, (((0,), (0,)), ((), ())), preferred_element_type=F32)


def nt(a, b):
    return lax.dot_general(a, b, (((1,), (1,)), ((), ())), preferred_element_type=F32)


def exact(a, b):
    return jnp.dot(a, b, preferred_element_type=F32, precision=HIGH)


def grid2(n, m):
    return (
        lax.broadcasted_iota(jnp.int32, (n, m), 0),
        lax.broadcasted_iota(jnp.int32, (n, m), 1),
    )


def onehot(mask, dtype=BF):
    return jnp.where(mask, 1.0, 0.0).astype(dtype)


def swap_lane(m):
    return ((m >> 5) & 3) * 128 + (m >> 7) * 32 + (m & 31)


def kernel(
    x_ref, c_ref, w_ref, ff_ref, mf_ref, lf_ref,
    dt_ref, gg_ref, gf_ref, gm_ref, gl_ref,
    zs_f, zr_f, zs_d, zr_d, ps_f, pr_f, ps_d, pr_d,
    ps_m, pr_m, zs_m, zr_m, ps_b, pr_b, zs_b, zr_b,
    xtj, ctj, gate, bk, bj, pm, pmt, pkj, aj, ajt, xg, fog, mbg, lbg, mid, loj, dj, dpt, gterm, gfold,
    ps_g, pr_g, zs_g, zr_g, row_g, ar_g,
    ps_s, pr_s, row_s, zr_s, head_s, ar_s,
    zss, zrs, pss, prs,
):
    g = lax.axis_index("grp")
    s = lax.axis_index("seq")
    z = s // 2
    y = s % 2
    p = y * 16 + g
    head = z // 4

    def z_id(t):
        return {"seq": t * 2 + y}

    def p_id(q):
        return {"grp": q % 16, "seq": z * 2 + q // 16}

    bar = pltpu.get_barrier_semaphore()

    def greet_z(d, _):
        pl.semaphore_signal(bar, inc=1, device_id=z_id((z + d) % 16), device_id_type=MESH)
        return _

    def greet_p(d, _):
        pl.semaphore_signal(bar, inc=1, device_id=p_id((p + d) % 32), device_id_type=MESH)
        return _

    lax.fori_loop(1, 16, greet_z, 0)
    lax.fori_loop(1, 32, greet_p, 0)

    def z_send(src, dst, rows, k):
        def step(d, _):
            t = (z + d) % 16
            pltpu.make_async_remote_copy(
                src_ref=src.at[pl.ds(pl.multiple_of(t * rows, rows), rows)],
                dst_ref=dst.at[pl.ds(pl.multiple_of(z * rows, rows), rows)],
                send_sem=zss.at[k], recv_sem=zrs.at[k],
                device_id=z_id(t), device_id_type=MESH,
            ).start()
            return _

        lax.fori_loop(1, 16, step, 0)
        mine = pl.ds(pl.multiple_of(z * rows, rows), rows)
        pltpu.make_async_copy(src.at[mine], dst.at[mine], zrs.at[k]).start()

    def z_cast(src, dst, k):
        def step(d, _):
            t = (z + d) % 16
            pltpu.make_async_remote_copy(
                src_ref=src, dst_ref=dst.at[z],
                send_sem=zss.at[k], recv_sem=zrs.at[k],
                device_id=z_id(t), device_id_type=MESH,
            ).start()
            return _

        lax.fori_loop(1, 16, step, 0)
        pltpu.make_async_copy(src, dst.at[z], zrs.at[k]).start()

    def p_send(src, dst, rows, k):
        def step(d, _):
            q = (p + d) % 32
            pltpu.make_async_remote_copy(
                src_ref=src.at[pl.ds(pl.multiple_of(q * rows, rows), rows)],
                dst_ref=dst.at[pl.ds(pl.multiple_of(p * rows, rows), rows)],
                send_sem=pss.at[k], recv_sem=prs.at[k],
                device_id=p_id(q), device_id_type=MESH,
            ).start()
            return _

        lax.fori_loop(1, 32, step, 0)
        mine = pl.ds(pl.multiple_of(p * rows, rows), rows)
        pltpu.make_async_copy(src.at[mine], dst.at[mine], prs.at[k]).start()

    def got(dst, sem):
        pltpu.make_async_copy(dst, dst, sem).wait()

    def sent(src, n, sem):
        part = src.at[pl.ds(0, n)]
        pltpu.make_async_copy(part, part, sem).wait()

    r, c = grid2(512, 512)
    bk[...] = onehot(r == (c & 31) * 16 + ((c >> 5) & 3) * 4 + (c >> 7))
    xtk = tn(x_ref[...], bk[...]).astype(BF)
    zs_f[0] = xtk[:, :256]
    zs_f[1] = xtk[:, 256:]
    pl.semaphore_wait(bar, 46)
    z_send(zs_f.at[0], zr_f.at[0], 32, 0)
    z_send(zs_f.at[1], zr_f.at[1], 32, 1)

    bj[...] = onehot(r == (c & 31) * 16 + (c >> 7) * 4 + ((c >> 5) & 3))
    xtj[...] = tn(x_ref[...], bj[...]).astype(BF)
    ctj[...] = tn(c_ref[...], bj[...]).astype(BF)
    gt = jax.nn.sigmoid(tn(w_ref[...], xtj[...]))
    gate[...] = gt
    dmix = (ctj[...].astype(F32) * gt).astype(BF)
    zs_d[0] = dmix[:, :256]
    zs_d[1] = dmix[:, 256:]
    z_send(zs_d.at[0], zr_d.at[0], 32, 2)
    z_send(zs_d.at[1], zr_d.at[1], 32, 3)

    pm[...] = onehot(c == (r & 15) * 32 + (r >> 4))
    pmt[...] = onehot(r == (c & 15) * 32 + (c >> 4))
    pkj[...] = onehot(r == swap_lane(c))
    r4, c4 = grid2(128, 32)
    spread4 = onehot((r4 & 31) == c4)
    r1, c1 = grid2(128, 128)
    same4 = (r1 >> 5) == (c1 >> 5)
    ff = ff_ref[head]
    half = mm(spread4, ff).astype(BF)
    fk = jnp.where(same4, nt(half, spread4), 0.0).astype(BF)
    half_t = nt(spread4, ff).astype(BF)
    fkt = jnp.where(same4, nt(half_t, spread4), 0.0).astype(BF)
    qk = onehot(c1 == (r1 & 15) * 8 + ((r1 >> 4) & 1) * 4 + (r1 >> 5))
    lf = lf_ref[head]
    lp = nt(mm(qk, lf).astype(BF), qk).astype(BF)
    lpt = nt(nt(qk, lf).astype(BF), qk).astype(BF)
    rj, cj = grid2(1024, 64)
    spread_j = onehot(cj == ((rj >> 4) & 15) * 4 + (rj >> 8))
    mf = mf_ref[head]
    wide = mm(spread_j, mf).astype(BF)
    wide_t = nt(spread_j, mf).astype(BF)
    for b in range(4):
        rows = slice(b * 256, b * 256 + 256)
        rb, cb = grid2(256, 1024)
        same16 = (rb & 15) == (cb & 15)
        aj[rows] = jnp.where(same16, nt(wide[rows], spread_j), 0.0).astype(BF)
        ajt[rows] = jnp.where(same16, nt(wide_t[rows], spread_j), 0.0).astype(BF)

    for ch in range(2):
        got(zr_f.at[ch], zrs.at[ch])
        ps_f[ch] = mm(pm[...], zr_f[ch]).astype(BF)
        p_send(ps_f.at[ch], pr_f.at[ch], 16, ch)

    for ch in range(2):
        got(pr_f.at[ch], prs.at[ch])
    for k in range(4):
        for yy in range(2):
            at = (k * 2 + yy) * 16
            xg[:, at : at + 16, :] = pr_f[
                k // 2, yy * 256 : yy * 256 + 256, (k % 2) * 128 : (k % 2) * 128 + 128
            ].reshape(16, 16, 128)
    fog[...] = mm(xg[...].reshape(2048, 128), fkt).astype(BF).reshape(16, 128, 128)
    for gi in range(16):
        lbg[gi] = mm(lp, fog[gi]).astype(BF)
    for k in range(4):
        for yy in range(2):
            at = (k * 2 + yy) * 16
            mid[yy * 256 : yy * 256 + 256, k * 128 : k * 128 + 128] = lbg[:, at : at + 16, :].reshape(256, 128)
    lo = mm(mid[...], pkj[...]).astype(BF)
    for j in range(4):
        for yy in range(2):
            loj[j * 256 : j * 256 + 256, yy * 128 : yy * 128 + 128] = lo[
                yy * 256 : yy * 256 + 256, j * 128 : j * 128 + 128
            ]
    for ch in range(2):
        mx = mm(aj[ch * 512 : ch * 512 + 512], loj[...]).astype(BF)
        for j in range(2):
            for yy in range(2):
                ps_m[ch, yy * 256 : yy * 256 + 256, j * 128 : j * 128 + 128] = mx[
                    j * 256 : j * 256 + 256, yy * 128 : yy * 128 + 128
                ]
        p_send(ps_m.at[ch], pr_m.at[ch], 16, 2 + ch)

    def d_relay(ch):
        got(zr_d.at[ch], zrs.at[2 + ch])
        ps_d[ch] = mm(pm[...], zr_d[ch]).astype(BF)
        p_send(ps_d.at[ch], pr_d.at[ch], 16, 4 + ch)

    d_relay(0)
    for ch in range(2):
        got(pr_m.at[ch], prs.at[2 + ch])
        zs_m[ch] = mm(pmt[...], pr_m[ch]).astype(BF)
        z_send(zs_m.at[ch], zr_m.at[ch], 32, 4 + ch)
    d_relay(1)

    for ch in range(2):
        got(pr_d.at[ch], prs.at[4 + ch])
    for j in range(4):
        for yy in range(2):
            dj[j * 256 : j * 256 + 256, yy * 128 : yy * 128 + 128] = pr_d[
                j // 2, yy * 256 : yy * 256 + 256, (j % 2) * 128 : (j % 2) * 128 + 128
            ]
    mb = mm(ajt[...], dj[...]).astype(BF)
    for j in range(4):
        for yy in range(2):
            mid[yy * 256 : yy * 256 + 256, j * 128 : j * 128 + 128] = mb[
                j * 256 : j * 256 + 256, yy * 128 : yy * 128 + 128
            ]
    mbk = mm(mid[...], pkj[...]).astype(BF)
    for k in range(4):
        for yy in range(2):
            at = (k * 2 + yy) * 16
            mbg[:, at : at + 16, :] = mbk[yy * 256 : yy * 256 + 256, k * 128 : k * 128 + 128].reshape(16, 16, 128)
    for gi in range(16):
        lbg[gi] = mm(lpt, mbg[gi]).astype(BF)
    fb = mm(lbg[...].reshape(2048, 128), fk).astype(BF).reshape(16, 128, 128)
    for ch in range(2):
        for k in range(2):
            for yy in range(2):
                at = ((ch * 2 + k) * 2 + yy) * 16
                ps_b[ch, yy * 256 : yy * 256 + 256, k * 128 : k * 128 + 128] = fb[:, at : at + 16, :].reshape(256, 128)
        p_send(ps_b.at[ch], pr_b.at[ch], 16, 6 + ch)

    for b in range(4):
        rb, cb = grid2(256, 1024)
        gram = nt(dj[b * 256 : b * 256 + 256], loj[...])
        gram = jnp.where((rb & 15) == (cb & 15), gram, 0.0)
        gfold[b * 16 : b * 16 + 16] = gram.reshape(16, 16, 1024).sum(axis=1)
    gm = exact(gfold[...], onehot(cj == ((rj >> 4) & 15) * 4 + (rj >> 8), F32))
    gl = jnp.zeros((128, 128), F32)
    gf = jnp.zeros((128, 128), F32)
    for gi in range(16):
        gl = gl + nt(mbg[gi], fog[gi])
        gf = gf + tn(lbg[gi], xg[gi])
    ra, ca = grid2(256, 128)
    pa, aa = ra >> 3, ra & 7
    kc = (ca & 15) * 8 + ((ca >> 4) & 1) * 4 + (ca >> 5)
    sel_l = onehot((aa < 4) & (kc == pa * 4 + aa), F32)
    pack = exact(sel_l, exact(gl, qk.astype(F32)))
    rm, cm = grid2(256, 64)
    jm = (cm & 15) * 4 + (cm >> 4)
    i64r, i64c = grid2(64, 128)
    for odd in range(2):
        sel_m = onehot(((rm & 7) == 4) & (jm == (rm >> 3) * 2 + odd), F32)
        pack = pack + exact(exact(sel_m, gm), onehot(i64c == i64r + 64 * odd, F32))
    fr, fc = grid2(256, 128)
    sel_f = onehot(((fr & 7) == 5) & ((fc & 31) == (fr >> 3)), F32)
    fold_c = onehot((c1 < 32) & ((r1 & 31) == c1), F32)
    pack = pack + exact(exact(sel_f, jnp.where(same4, gf, 0.0)), fold_c)
    ps_s[...] = pack
    p_send(ps_s, pr_s, 8, 8)

    for ch in range(2):
        got(pr_b.at[ch], prs.at[6 + ch])
        zs_b[ch] = mm(pmt[...], pr_b[ch]).astype(BF)
        z_send(zs_b.at[ch], zr_b.at[ch], 32, 6 + ch)

    got(pr_s, prs.at[8])
    row_s[...] = pr_s[...].reshape(32, 8, 128).sum(axis=0)
    z_cast(row_s, zr_s, 8)

    for ch in range(2):
        got(zr_m.at[ch], zrs.at[4 + ch])
        cols = slice(ch * 256, ch * 256 + 256)
        gt = gate[:, cols]
        dpt[:, cols] = (
            ctj[:, cols].astype(F32) * zr_m[ch].astype(F32) * gt * (1.0 - gt)
        ).astype(BF)
    ps_g[...] = nt(mm(pm[...], xtj[...]).astype(BF), dpt[...]).astype(ps_g.dtype)
    p_send(ps_g, pr_g, 16, 9)
    gterm[...] = nt(nt(bj[...], dpt[...]).astype(BF), w_ref[...])

    got(zr_s, zrs.at[8])
    head_s[...] = zr_s[...].reshape(4, 4, 8, 128).sum(axis=1).reshape(32, 128) * SCALE

    def a_send(d, _):
        q = (p + d) % 32
        pltpu.make_async_remote_copy(
            src_ref=head_s, dst_ref=ar_s.at[p],
            send_sem=pss.at[10], recv_sem=prs.at[10],
            device_id=p_id(q), device_id_type=MESH,
        ).start()
        return _

    lax.fori_loop(1, 32, a_send, 0)
    pltpu.make_async_copy(head_s, ar_s.at[p], prs.at[10]).start()

    got(pr_g, prs.at[9])
    tot = pr_g[...].astype(F32).reshape(32, 16, 512).sum(axis=0)
    for t in range(16):
        zs_g[t] = tot[t : t + 1]
    z_send(zs_g, zr_g, 1, 9)

    got(ar_s, prs.at[10])
    for h in range(4):
        gl_ref[h] = ar_s[s, h * 8 : h * 8 + 4, :]
        for a in range(2):
            both = ar_s[g * 2 + a, h * 8 + 4 : h * 8 + 5, :]
            gm_ref[h, a * 2 : a * 2 + 1, :] = both[:, :64]
            gm_ref[h, a * 2 + 1 : a * 2 + 2, :] = both[:, 64:]
        for q in range(32):
            gf_ref[h, q : q + 1, :] = ar_s[q, h * 8 + 5 : h * 8 + 6, :32]

    got(zr_g, zrs.at[9])
    row_g[...] = zr_g[...].sum(axis=0) * SCALE

    def ag_send(d, _):
        q = (g + d) % 16
        pltpu.make_async_remote_copy(
            src_ref=row_g, dst_ref=ar_g.at[g],
            send_sem=pss.at[11], recv_sem=prs.at[11],
            device_id={"grp": q}, device_id_type=MESH,
        ).start()
        return _

    lax.fori_loop(1, 16, ag_send, 0)
    pltpu.make_async_copy(row_g, ar_g.at[g], prs.at[11]).start()

    for ch in range(2):
        got(zr_b.at[ch], zrs.at[6 + ch])
    back = nt(bk[:, :256], zr_b[0]) + nt(bk[:, 256:], zr_b[1])
    dt_ref[...] = (back + gterm[...]).astype(BF)

    got(ar_g, prs.at[11])
    for q in range(16):
        gg_ref[q : q + 1] = ar_g[q]

    for ch in range(2):
        for k, src in enumerate((zs_f, zs_d, zs_m, zs_b)):
            sent(src.at[ch], 480, zss.at[k * 2 + ch])
        for k, src in enumerate((ps_f, ps_m, ps_d, ps_b)):
            sent(src.at[ch], 496, pss.at[k * 2 + ch])
    sent(zr_s, 15, zss.at[8])
    sent(zs_g, 15, zss.at[9])
    sent(ps_s, 248, pss.at[8])
    sent(ps_g, 496, pss.at[9])
    sent(ar_s, 31, pss.at[10])
    sent(ar_g, 15, pss.at[11])


def shards(tokens, cotangent, gate_weight, first_factor, middle_factor, last_factor):
    V = pltpu.VMEM
    big = V((2, 512, 256), BF)
    sq = V((512, 512), BF)
    gtype = BF
    scratch = (
        [big] * 16
        + [sq, sq, V((512, 512), F32), sq, sq, sq, sq, sq, V((1024, 1024), BF), V((1024, 1024), BF)]
        + [V((16, 128, 128), BF)] * 4
        + [sq, V((1024, 256), BF), V((1024, 256), BF), sq, V((512, 512), F32), V((64, 1024), F32)]
        + [V((512, 512), gtype)] * 2
        + [V((16, 1, 512), F32), V((16, 1, 512), F32), V((1, 512), F32), V((16, 1, 512), F32)]
        + [V((256, 128), F32)] * 2
        + [V((8, 128), F32), V((16, 8, 128), F32), V((32, 128), F32), V((32, 32, 128), F32)]
        + [pltpu.SemaphoreType.DMA((12,))] * 4
    )
    vm = pl.BlockSpec(memory_space=V)
    dt, gg, gf, gm, gl = pl.pallas_call(
        kernel,
        name="mixer",
        out_shape=(
            jax.ShapeDtypeStruct((512, 512), BF),
            jax.ShapeDtypeStruct((16, 512), F32),
            jax.ShapeDtypeStruct((4, 32, 32), F32),
            jax.ShapeDtypeStruct((4, 4, 64), F32),
            jax.ShapeDtypeStruct((4, 4, 128), F32),
        ),
        in_specs=[vm] * 6,
        out_specs=(vm,) * 5,
        scratch_shapes=scratch,
        compiler_params=pltpu.CompilerParams(
            collective_id=0, has_side_effects=True, vmem_limit_bytes=60 * 1024 * 1024
        ),
    )(
        tokens.reshape(512, 512), cotangent.reshape(512, 512),
        gate_weight, first_factor, middle_factor, last_factor,
    )
    return dt.reshape(tokens.shape), gg, gf, gm, gl


def solution(mesh):
    in_specs = (P(None, "grp", "seq", None), P(None, "grp", "seq", None), P(), P(), P(), P())
    out_specs = (
        P(None, "grp", "seq", None),
        P("seq", None),
        P(),
        P(None, "grp", None),
        P(None, "seq", None),
    )
    return jax.shard_map(shards, mesh=mesh, in_specs=in_specs, out_specs=out_specs, check_vma=False)
```

time: 430 us -> 142 us (0.33)
  waiting for transfers between devices: 174 us -> 0 us
  blocking collectives: 137 us -> 0 us
  Pallas kernels: 0 us -> 133 us
  starting transfers between devices: 58.9 us -> 0 us
  local copies, waits for them, and re-layouts: 29 us -> 7.75 us
  between operations: 14.5 us -> 0.66 us
  matrix products: 8.62 us -> 0 us
  other arithmetic: 5.13 us -> 0 us
    all_to_all x5 -> x0, blocking collectives: 137 us -> none  [the longest x2 83.8 us: send_last(): lax.all_to_all(values, 'seq', split_axis=0, concat_axis=2, tiled=True)]
    pallas_call x0 -> x1, Pallas kernels: none -> 133 us  [shards(): pl.pallas_call(kernel, name='mixer', out_shape=(jax.ShapeDtypeStruct((512...]
    all_to_all x6 -> x0, waiting for transfers between devices: 110 us -> none  [the longest x2 56.7 us: return_last(): lax.all_to_all(values, 'seq', split_axis=2, concat_axis=0, tiled=True)]
    reduce_scatter x1 -> x0, waiting for transfers between devices: 63.6 us -> none  [sum_together(): lax.psum_scatter(lines, axis, tiled=True).reshape(-1)]
    all_to_all x6 -> x0, starting transfers between devices: 58.7 us -> none  [the longest x2 38.8 us: copy_for_each(): return lax.all_to_all(copies, axis, split_axis=0, concat_axis=0, tiled=True)]
    dot_general x12 -> x0, matrix products: 8.62 us -> none  [the longest x6 3.69 us: mixing(): jnp.einsum(form, weights, headed(values), preferred_element_type=jnp.floa...]
    convert_element_type x10 -> x0, local copies, waits for them, and re-layouts: 4.56 us -> none  [the longest x2 1.23 us: shards(): mixing(last_factor, last_back_in, 'hba,ijbhe->ijahe').astype(jnp.bfloat16)]
    all_to_all x10 -> x0, local copies, waits for them, and re-layouts: 4.33 us -> none  [the longest x3 3.12 us: return_middle(): lax.all_to_all(values, 'grp', split_axis=1, concat_axis=2, tiled=True)]
  transfers between devices with their start and end apart: 7 -> 0, of which waited for: 6 -> 0; matrix products, arithmetic and copies ran while one was open for 4% -> 0% of each run, Pallas kernels for 0% -> 0%
where the time goes in v1:
time: 142 us; the launch traced here: 141 us
  Pallas kernels  133 us (94%)
  local copies, waits for them, and re-layouts  7.75 us (5%)
    pallas_call x1, Pallas kernels, shards(): pl.pallas_call(kernel, name='mixer', out_shape=(jax.ShapeDtypeStruct((512...  133 us
    unnamed x14, local copies, waits for them, and re-layouts  2.85 us

profile of v1, /device:TPU:1, one launch (start us, length us, event | category | flops | bytes accessed | tf_op | source)
XLA Modules:
  0.0 141.3 jit_solution(8613917787453940270)
XLA Ops:
  0.6 0.0 copy-start
  0.6 2.0 %reshape.19.x_ref = bf16[512,512]{1,0:T(8,128)(2,1)} reshape(bf16[32,4,4,512]{3,2,1,0:T(4,128)(2,1)} %param.6) | data formatting | bytes 1048576 | tf_op jit(solution)/shard_map/reshape | solution.py:406
  2.7 0.0 copy-done
  2.7 0.9 reshape.20.c_ref
  3.6 132.8 %mixer.1 = (bf16[512,512]{1,0:T(8,128)(2,1)}, f32[16,512]{1,0:T(8,128)}, f32[4,32,32]{2,1,0:T(8,128)}, f32[4,4,64]{2,1,0:T(4,128)}, f32[4,4,128]{2,1,0:T(4,128)}) custom-call(bf16[512,512]{1,0:T(8,128)(2,1)} %reshape.19.x_ref, bf16[512,512]{1,0:T(8,128)(2,1)} %reshape.20.c_ref, bf16[512,512]{1,0:T(8,128)(2,1)} %w_ref.1, bf16[4,32,32]{2,1,0:T(8,128)(2,1)} %ff_ref.1, ...), custom_call_target="tpu_custom_call" | custom-call | tf_op jit(solution)/shard_map/mixer/pallas_call | solution.py:389
  136.4 0.0 copy-start.2
  136.4 2.0 %reshape.21 = bf16[32,4,4,512]{3,2,1,0:T(4,128)(2,1)} reshape(bf16[512,512]{1,0:T(8,128)(2,1)} %get-tuple-element.10) | data formatting | bytes 1048576 | tf_op jit(solution)/shard_map/reshape | solution.py:409
  138.4 0.0 copy-done.2
  138.4 0.0 copy-start.1
  138.4 0.6 copy.15
  139.0 0.2 copy-done.1
  139.3 0.0 copy-start.4
  139.3 0.6 copy.16
  139.9 0.1 copy-done.4
  140.0 0.0 copy-start.3
  140.0 0.6 copy.17
  140.6 0.1 copy-done.3
  140.7 0.6 copy.18
Async XLA Ops:
  0.6 2.0 %copy-start = (bf16[32,4,4,512]{3,2,1,0:T(4,128)(2,1)S(1)}, bf16[32,4,4,512]{3,2,1,0:T(4,128)(2,1)}, u32[]{:S(2)}) copy-start(bf16[32,4,4,512]{3,2,1,0:T(4,128)(2,1)} %param.7) | copy-start | bytes 1572868
  136.4 2.0 %copy-start.2 = (f32[16,512]{1,0:T(8,128)S(1)}, f32[16,512]{1,0:T(8,128)}, u32[]{:S(2)}) copy-start(f32[16,512]{1,0:T(8,128)} %get-tuple-element.21) | copy-start | bytes 98308
  138.4 0.9 copy-start.1
  139.3 0.7 copy-start.4
  140.0 0.7 copy-start.3

commit v2 on v1

v2 whole, which is shorter than its diff:
```python
import jax
import jax.numpy as jnp
from jax import lax
from jax.experimental import pallas as pl
from jax.experimental.pallas import tpu as pltpu
from jax.sharding import PartitionSpec as P

MESH = pl.DeviceIdType.MESH
BF = jnp.bfloat16
F32 = jnp.float32
SCALE = 1.0 / 512.0
HIGH = lax.Precision.HIGHEST
SPLIT = 8


def mm(a, b):
    return jnp.dot(a, b, preferred_element_type=F32)


def tn(a, b):
    return lax.dot_general(a, b, (((0,), (0,)), ((), ())), preferred_element_type=F32)


def nt(a, b):
    return lax.dot_general(a, b, (((1,), (1,)), ((), ())), preferred_element_type=F32)


def exact(a, b):
    return jnp.dot(a, b, preferred_element_type=F32, precision=HIGH)


def grid2(n, m):
    return (
        lax.broadcasted_iota(jnp.int32, (n, m), 0),
        lax.broadcasted_iota(jnp.int32, (n, m), 1),
    )


def onehot(mask, dtype=BF):
    return jnp.where(mask, 1.0, 0.0).astype(dtype)


def swap_lane(m):
    return ((m >> 5) & 3) * 128 + (m >> 7) * 32 + (m & 31)


def kernel(
    x_in, c_in, w_in, ff_in, mf_in, lf_in,
    dt_ref, gg_ref, sm_ref,
    x_ref, c_ref, w_ref, ff_ref, mf_ref, lf_ref,
    zs_f, zr_f, zs_d, zr_d, ps_f, pr_f, ps_d, pr_d,
    ps_m, pr_m, zs_m, zr_m, ps_b, pr_b, zs_b, zr_b,
    xn, xtj, ctj, gate, bk, bj, pm, pmt, pkj, mid, dpt, xtp, gterm,
    aj, ajt, loj, dj, xg, fog, mbg, lbg, gfold, gacc,
    ps_g, pr_g, zs_g, zr_g, row_g, ar_g,
    ps_s, pr_s, row_s, zr_s, row_l, zr_l, few_s, ar_s, big_s, ar_l,
    zss, zrs, pss, prs, ins,
):
    g = lax.axis_index("grp")
    s = lax.axis_index("seq")
    z = lax.div(s, 2)
    y = lax.rem(s, 2)
    p = y * 16 + g
    head = lax.div(z, 4)

    def z_id(t):
        return {"seq": t * 2 + y}

    def p_id(q):
        return {"grp": lax.rem(q, 16), "seq": z * 2 + lax.div(q, 16)}

    def around(d):
        return lax.rem(z + d, 16)

    loads = [
        pltpu.make_async_copy(src, dst, ins.at[n])
        for n, (src, dst) in enumerate(
            ((x_in, x_ref), (c_in, c_ref), (w_in, w_ref), (ff_in, ff_ref), (mf_in, mf_ref), (lf_in, lf_ref))
        )
    ]
    for load in loads:
        load.start()
    bar = pltpu.get_barrier_semaphore()
    waiting, leaving = {}, []

    def greet_z(d, _):
        pl.semaphore_signal(bar, inc=1, device_id=z_id(around(d)), device_id_type=MESH)
        return _

    def greet_p(d, _):
        pl.semaphore_signal(bar, inc=1, device_id=p_id(lax.rem(p + d, 32)), device_id_type=MESH)
        return _

    lax.fori_loop(1, 16, greet_z, 0)
    lax.fori_loop(1, 32, greet_p, 0)

    def block(t, rows):
        return pl.ds(pl.multiple_of(t * rows, rows), rows)

    def z_send(src, dst, rows, k, first=1, last=16):
        def step(d, _):
            t = around(d * 7)
            pltpu.make_async_remote_copy(
                src_ref=src.at[block(t, rows)], dst_ref=dst.at[block(z, rows)],
                send_sem=zss.at[k], recv_sem=zrs.at[k],
                device_id=z_id(t), device_id_type=MESH,
            ).start()
            return _

        lax.fori_loop(first, last, step, 0)
        if last < 16:
            return
        pltpu.make_async_copy(src.at[block(z, rows)], dst.at[block(z, rows)], zrs.at[k]).start()
        note(dst, zrs, k)
        note_sent(src, 15 * rows, zss.at[k])

    def p_send(src, dst, rows, k):
        def step(d, _):
            q = lax.rem(p + d * 13, 32)
            pltpu.make_async_remote_copy(
                src_ref=src.at[block(q, rows)], dst_ref=dst.at[block(p, rows)],
                send_sem=pss.at[k], recv_sem=prs.at[k],
                device_id=p_id(q), device_id_type=MESH,
            ).start()
            return _

        lax.fori_loop(1, 32, step, 0)
        pltpu.make_async_copy(src.at[block(p, rows)], dst.at[block(p, rows)], prs.at[k]).start()
        note(dst, prs, k)
        note_sent(src, 31 * rows, pss.at[k])

    def got(dst, sem, n):
        pltpu.make_async_copy(dst, dst, sem.at[n]).wait()
        waiting.pop((id(sem), n), None)

    def note(dst, sem, n):
        waiting[(id(sem), n)] = lambda: got(dst, sem, n)

    def note_sent(src, n, sem):
        part = src.at[pl.ds(0, n)]
        leaving.append(pltpu.make_async_copy(part, part, sem))

    def finish():
        for step in list(waiting.values()):
            step()
        for copy in leaving:
            copy.wait()

    def lanes(j):
        return slice(j * 128, j * 128 + 128)

    def half(yy):
        return slice(yy * 256, yy * 256 + 256)

    r, c = grid2(512, 512)
    bk[...] = onehot(r == (c & 31) * 16 + ((c >> 5) & 3) * 4 + (c >> 7))
    loads[0].wait()
    xn[...] = x_ref[...].reshape(512, 512)
    xtk = tn(xn[...], bk[...]).astype(BF)
    for k in range(4):
        zs_f[k] = xtk[:, lanes(k)]
    pl.semaphore_wait(bar, 46)
    for k in range(4):
        z_send(zs_f.at[k], zr_f.at[k], 32, k)

    bj[...] = onehot(r == (c & 31) * 16 + (c >> 7) * 4 + ((c >> 5) & 3))
    xtj[...] = tn(xn[...], bj[...]).astype(BF)
    loads[1].wait()
    ctj[...] = tn(c_ref[...].reshape(512, 512), bj[...]).astype(BF)
    loads[2].wait()
    gt = jax.nn.sigmoid(tn(w_ref[...], xtj[...]))
    gate[...] = gt
    dmix = (ctj[...].astype(F32) * gt).astype(BF)
    for j in range(4):
        zs_d[j] = dmix[:, lanes(j)]
    for j in range(4):
        z_send(zs_d.at[j], zr_d.at[j], 32, 4 + j)

    pm[...] = onehot(c == (r & 15) * 32 + (r >> 4))
    pmt[...] = onehot(r == (c & 15) * 32 + (c >> 4))
    pkj[...] = onehot(r == swap_lane(c))
    r4, c4 = grid2(128, 32)
    spread4 = onehot((r4 & 31) == c4)
    r1, c1 = grid2(128, 128)
    same4 = (r1 >> 5) == (c1 >> 5)
    for load in loads[3:]:
        load.wait()
    ff = ff_ref[head]
    fk = jnp.where(same4, nt(mm(spread4, ff).astype(BF), spread4), 0.0).astype(BF)
    fkt = jnp.where(same4, nt(nt(spread4, ff).astype(BF), spread4), 0.0).astype(BF)
    qk = onehot(c1 == (r1 & 15) * 8 + ((r1 >> 4) & 1) * 4 + (r1 >> 5))
    lf = lf_ref[head]
    lp = nt(mm(qk, lf).astype(BF), qk).astype(BF)
    lpt = nt(nt(qk, lf).astype(BF), qk).astype(BF)
    rj, cj = grid2(1024, 64)
    spread_j = onehot(cj == ((rj >> 4) & 15) * 4 + (rj >> 8))
    mf = mf_ref[head]
    wide = mm(spread_j, mf).astype(BF)
    wide_t = nt(spread_j, mf).astype(BF)
    for b in range(4):
        rb, cb = grid2(256, 1024)
        same16 = (rb & 15) == (cb & 15)
        aj[half(b)] = jnp.where(same16, nt(wide[half(b)], spread_j), 0.0).astype(BF)
        ajt[half(b)] = jnp.where(same16, nt(wide_t[half(b)], spread_j), 0.0).astype(BF)
    xtp[...] = mm(pm[...], xtj[...]).astype(BF)

    for k in range(4):
        got(zr_f.at[k], zrs, k)
        ps_f[k] = mm(pm[...], zr_f[k]).astype(BF)
        p_send(ps_f.at[k], pr_f.at[k], 16, k)

    for k in range(4):
        got(pr_f.at[k], prs, k)
        fo = mm(pr_f[k], fkt).astype(BF)
        for yy in range(2):
            at = (k * 2 + yy) * 16
            fog[:, at : at + 16, :] = fo[half(yy)].reshape(16, 16, 128)
    for gi in range(16):
        lbg[gi] = mm(lp, fog[gi]).astype(BF)
    for k in range(4):
        for yy in range(2):
            at = (k * 2 + yy) * 16
            mid[half(yy), lanes(k)] = lbg[:, at : at + 16, :].reshape(256, 128)
    lo = mm(mid[...], pkj[...]).astype(BF)
    for j in range(4):
        for yy in range(2):
            loj[half(j), lanes(yy)] = lo[half(yy), lanes(j)]
    for j in range(4):
        mx = mm(aj[half(j)], loj[...]).astype(BF)
        for yy in range(2):
            ps_m[j, half(yy)] = mx[:, lanes(yy)]
        p_send(ps_m.at[j], pr_m.at[j], 16, 4 + j)

    def d_relay(j):
        got(zr_d.at[j], zrs, 4 + j)
        ps_d[j] = mm(pm[...], zr_d[j]).astype(BF)
        p_send(ps_d.at[j], pr_d.at[j], 16, 8 + j)

    def m_relay(j):
        got(pr_m.at[j], prs, 4 + j)
        zs_m[j] = mm(pmt[...], pr_m[j]).astype(BF)
        z_send(zs_m.at[j], zr_m.at[j], 32, 8 + j)

    d_relay(0)
    d_relay(1)
    m_relay(0)
    d_relay(2)
    m_relay(1)
    m_relay(2)
    d_relay(3)
    m_relay(3)

    for j in range(4):
        got(pr_d.at[j], prs, 8 + j)
        for yy in range(2):
            dj[half(j), lanes(yy)] = pr_d[j, half(yy)]
    mb = mm(ajt[...], dj[...]).astype(BF)
    for j in range(4):
        for yy in range(2):
            mid[half(yy), lanes(j)] = mb[half(j), lanes(yy)]
    mbk = mm(mid[...], pkj[...]).astype(BF)
    for k in range(4):
        for yy in range(2):
            at = (k * 2 + yy) * 16
            mbg[:, at : at + 16, :] = mbk[half(yy), lanes(k)].reshape(16, 16, 128)
    for gi in range(16):
        lbg[gi] = mm(lpt, mbg[gi]).astype(BF)
    fb = mm(lbg[...].reshape(2048, 128), fk).astype(BF).reshape(16, 128, 128)
    for k in range(4):
        for yy in range(2):
            at = (k * 2 + yy) * 16
            ps_b[k, half(yy)] = fb[:, at : at + 16, :].reshape(256, 128)
    for k in range(2):
        p_send(ps_b.at[k], pr_b.at[k], 16, 12 + k)

    for k in range(4):
        for yy in range(2):
            at = (k * 2 + yy) * 16
            xg[:, at : at + 16, :] = pr_f[k, half(yy)].reshape(16, 16, 128)
    for b in range(4):
        rb, cb = grid2(256, 1024)
        gram = nt(dj[half(b)], loj[...])
        gram = jnp.where((rb & 15) == (cb & 15), gram, 0.0)
        gfold[b * 16 : b * 16 + 16] = gram.reshape(16, 16, 1024).sum(axis=1)
    gm = exact(gfold[...], onehot(cj == ((rj >> 4) & 15) * 4 + (rj >> 8), F32))
    gl = jnp.zeros((128, 128), F32)
    gf = jnp.zeros((128, 128), F32)
    for gi in range(16):
        gl = gl + nt(mbg[gi], fog[gi])
        gf = gf + tn(lbg[gi], xg[gi])
    ra, ca = grid2(256, 128)
    pa, aa = ra >> 3, ra & 7
    kc = (ca & 15) * 8 + ((ca >> 4) & 1) * 4 + (ca >> 5)
    sel_l = onehot((aa < 4) & (kc == pa * 4 + aa), F32)
    pack = exact(sel_l, exact(gl, qk.astype(F32)))
    rm, cm = grid2(256, 64)
    jm = (cm & 15) * 4 + (cm >> 4)
    i64r, i64c = grid2(64, 128)
    for odd in range(2):
        sel_m = onehot(((rm & 7) == 4) & (jm == (rm >> 3) * 2 + odd), F32)
        pack = pack + exact(exact(sel_m, gm), onehot(i64c == i64r + 64 * odd, F32))
    sel_f = onehot((aa == 5) & ((ca & 31) == pa), F32)
    fold_c = onehot(c1 == (r1 & 31) + head * 32, F32)
    pack = pack + exact(exact(sel_f, jnp.where(same4, gf, 0.0)), fold_c)
    ps_s[...] = pack
    p_send(ps_s, pr_s, 8, 16)
    for k in range(2, 4):
        p_send(ps_b.at[k], pr_b.at[k], 16, 12 + k)

    def b_relay(k):
        got(pr_b.at[k], prs, 12 + k)
        zs_b[k] = mm(pmt[...], pr_b[k]).astype(BF)
        z_send(zs_b.at[k], zr_b.at[k], 32, 12 + k)

    def gate_share(j):
        got(zr_m.at[j], zrs, 8 + j)
        gt = gate[:, lanes(j)]
        dpre = (ctj[:, lanes(j)].astype(F32) * zr_m[j].astype(F32) * gt * (1.0 - gt)).astype(BF)
        dpt[:, lanes(j)] = dpre
        share = nt(xtp[:, lanes(j)], dpre)
        if j == 0:
            gacc[...] = share
        elif j < 3:
            gacc[...] += share
        else:
            ps_g[...] = (gacc[...] + share).astype(BF)

    b_relay(0)
    gate_share(0)
    gate_share(1)
    b_relay(1)
    gate_share(2)
    gate_share(3)
    p_send(ps_g, pr_g, 16, 17)
    b_relay(2)

    owner = lax.div(p, 2) == z
    side = lax.rem(p, 2)
    got(pr_s, prs, 16)
    row = pr_s[...].reshape(32, 8, 128).sum(axis=0)
    row_s[...] = row[4:6]
    row_l[...] = row[0:4]

    def row_copy():
        return pltpu.make_async_remote_copy(
            src_ref=row_l, dst_ref=zr_l.at[z], send_sem=zss.at[18], recv_sem=zrs.at[18],
            device_id=z_id(lax.div(p, 2)), device_id_type=MESH,
        )

    @pl.when(owner)
    def _():
        pltpu.make_async_copy(row_l, zr_l.at[z], zrs.at[18]).start()

    @pl.when(jnp.logical_not(owner))
    def _():
        row_copy().start()

    def cast(d, _):
        pltpu.make_async_remote_copy(
            src_ref=row_s, dst_ref=zr_s.at[z], send_sem=zss.at[16], recv_sem=zrs.at[16],
            device_id=z_id(around(d)), device_id_type=MESH,
        ).start()
        return _

    lax.fori_loop(1, 16, cast, 0)
    pltpu.make_async_copy(row_s, zr_s.at[z], zrs.at[16]).start()
    note(zr_s, zrs, 16)
    note_sent(zr_s, 15, zss.at[16])

    got(pr_b.at[3], prs, 15)
    zs_b[3] = mm(pmt[...], pr_b[3]).astype(BF)
    z_send(zs_b.at[3], zr_b.at[3], 32, 15, 1, SPLIT)
    gterm[...] = nt(nt(bj[...], dpt[...]).astype(BF), w_ref[...])

    got(pr_g, prs, 17)
    tot = pr_g[...].astype(F32).reshape(32, 16, 512).sum(axis=0)
    for t in range(16):
        zs_g[t] = tot[t : t + 1]
    z_send(zs_g, zr_g, 1, 17)
    z_send(zs_b.at[3], zr_b.at[3], 32, 15, SPLIT, 16)

    got(zr_s, zrs, 16)
    for h in range(4):
        few_s[h : h + 1] = zr_s[4 * h : 4 * h + 4, 0:1, :].sum(axis=0) * SCALE
    few_s[4:5] = zr_s[:, 1:2, :].sum(axis=0) * SCALE
    few_s[5:8] = jnp.zeros((3, 128), F32)

    def few(d, _):
        q = lax.rem(p + d * 13, 32)
        pltpu.make_async_remote_copy(
            src_ref=few_s, dst_ref=ar_s.at[p], send_sem=pss.at[18], recv_sem=prs.at[18],
            device_id=p_id(q), device_id_type=MESH,
        ).start()
        return _

    lax.fori_loop(1, 32, few, 0)
    pltpu.make_async_copy(few_s, ar_s.at[p], prs.at[18]).start()
    note_sent(ar_s, 31, pss.at[18])

    def big_copy(t):
        return pltpu.make_async_remote_copy(
            src_ref=big_s, dst_ref=ar_l, send_sem=pss.at[19], recv_sem=prs.at[19],
            device_id={"grp": t, "seq": z * 2 + side}, device_id_type=MESH,
        )

    @pl.when(owner)
    def _():
        got(zr_l, zrs, 18)
        for h in range(4):
            big_s[h * 4 : h * 4 + 4] = zr_l[4 * h : 4 * h + 4].sum(axis=0) * SCALE

        def step(d, _):
            big_copy(lax.rem(g + d, 16)).start()
            return _

        lax.fori_loop(1, 16, step, 0)

    @pl.when(owner & (side == y))
    def _():
        pltpu.make_async_copy(big_s, ar_l, prs.at[19]).start()

    @pl.when(owner & (side != y))
    def _():
        big_copy(g).start()

    got(ar_l, prs, 19)
    sm_ref[0:16] = ar_l[...]
    got(ar_s, prs, 18)
    for a in range(2):
        sm_ref[16 + a * 4 : 20 + a * 4] = ar_s[g * 2 + a, 0:4, :]
    for q in range(32):
        sm_ref[24 + q : 25 + q] = ar_s[q, 4:5, :]

    got(zr_g, zrs, 17)
    row_g[...] = zr_g[...].sum(axis=0) * SCALE

    def rows_out(d, _):
        pltpu.make_async_remote_copy(
            src_ref=row_g, dst_ref=ar_g.at[g], send_sem=pss.at[20], recv_sem=prs.at[20],
            device_id={"grp": lax.rem(g + d, 16)}, device_id_type=MESH,
        ).start()
        return _

    lax.fori_loop(1, 16, rows_out, 0)
    pltpu.make_async_copy(row_g, ar_g.at[g], prs.at[20]).start()
    note_sent(ar_g, 15, pss.at[20])

    for k in range(3):
        got(zr_b.at[k], zrs, 12 + k)
        gterm[...] += nt(bk[:, lanes(k)], zr_b[k])
    got(zr_b.at[3], zrs, 15)
    dt_ref[...] = (gterm[...] + nt(bk[:, lanes(3)], zr_b[3])).astype(BF)

    got(ar_g, prs, 20)
    for q in range(16):
        gg_ref[q : q + 1] = ar_g[q]

    finish()

    @pl.when(jnp.logical_not(owner))
    def _():
        row_copy().wait_send()

    @pl.when(owner)
    def _():
        for _i in range(15):
            got(big_s, pss, 19)

    @pl.when(owner & (side != y))
    def _():
        got(big_s, pss, 19)


def unpack(dt_ref, gg_ref, sm_ref, d_ref, g_ref, f_ref, m_ref, l_ref):
    d_ref[...] = dt_ref[...].reshape(32, 4, 4, 512)
    g_ref[...] = gg_ref[...]
    for h in range(4):
        l_ref[h] = sm_ref[h * 4 : h * 4 + 4]
        for a in range(2):
            m_ref[h, a * 2 : a * 2 + 1] = sm_ref[16 + a * 4 + h : 17 + a * 4 + h, :64]
            m_ref[h, a * 2 + 1 : a * 2 + 2] = sm_ref[16 + a * 4 + h : 17 + a * 4 + h, 64:]
        f_ref[h] = sm_ref[24:56, h * 32 : h * 32 + 32]


def shards(tokens, cotangent, gate_weight, first_factor, middle_factor, last_factor):
    V = pltpu.VMEM
    big = V((4, 512, 128), BF)
    sq = V((512, 512), BF)
    scratch = (
        [V(a.shape, BF) for a in (tokens, cotangent, gate_weight, first_factor, middle_factor, last_factor)]
        + [big] * 16
        + [sq, sq, sq, V((512, 512), F32), sq, sq, sq, sq, sq, sq, sq, sq, V((512, 512), F32)]
        + [V((1024, 1024), BF)] * 2
        + [V((1024, 256), BF)] * 2
        + [V((16, 128, 128), BF)] * 4
        + [V((64, 1024), F32), V((512, 512), F32)]
        + [sq, sq, V((16, 1, 512), F32), V((16, 1, 512), F32), V((1, 512), F32), V((16, 1, 512), F32)]
        + [V((256, 128), F32)] * 2
        + [V((2, 128), F32), V((16, 2, 128), F32), V((4, 128), F32), V((16, 4, 128), F32), V((8, 128), F32), V((32, 8, 128), F32)]
        + [V((16, 128), F32)] * 2
        + [pltpu.SemaphoreType.DMA((n,)) for n in (19, 19, 21, 21, 6)]
    )
    vm = pl.BlockSpec(memory_space=V)
    dt, gg, sm = pl.pallas_call(
        kernel,
        name="mixer",
        out_shape=(
            jax.ShapeDtypeStruct((512, 512), BF),
            jax.ShapeDtypeStruct((16, 512), F32),
            jax.ShapeDtypeStruct((56, 128), F32),
        ),
        in_specs=[pl.BlockSpec(memory_space=pl.ANY)] * 6,
        out_specs=(vm,) * 3,
        scratch_shapes=scratch,
        compiler_params=pltpu.CompilerParams(
            collective_id=0, has_side_effects=True, vmem_limit_bytes=60 * 1024 * 1024
        ),
    )(tokens, cotangent, gate_weight, first_factor, middle_factor, last_factor)
    return pl.pallas_call(
        unpack,
        name="unpack",
        out_shape=(
            jax.ShapeDtypeStruct((32, 4, 4, 512), BF),
            jax.ShapeDtypeStruct((16, 512), F32),
            jax.ShapeDtypeStruct((4, 32, 32), F32),
            jax.ShapeDtypeStruct((4, 4, 64), F32),
            jax.ShapeDtypeStruct((4, 4, 128), F32),
        ),
        in_specs=[vm] * 3,
        out_specs=(vm,) * 5,
    )(dt, gg, sm)


def solution(mesh):
    in_specs = (P(None, "grp", "seq", None), P(None, "grp", "seq", None), P(), P(), P(), P())
    out_specs = (
        P(None, "grp", "seq", None),
        P("seq", None),
        P(),
        P(None, "grp", None),
        P(None, "seq", None),
    )
    return jax.shard_map(shards, mesh=mesh, in_specs=in_specs, out_specs=out_specs, check_vma=False)
```

time: 142 us -> 124 us (0.87)
  Pallas kernels: 133 us -> 123 us
  local copies, waits for them, and re-layouts: 7.75 us -> 0 us
    pallas_call x1, Pallas kernels: 133 us -> 121 us  [shards(): pl.pallas_call(kernel, name='mixer', out_shape=(jax.ShapeDtypeStruct((512...]
    reshape x3 -> x0, local copies, waits for them, and re-layouts: 4.89 us -> none  [the longest x1 2.02 us: shards(): tokens.reshape(512, 512)]
    unnamed x14 -> x0, local copies, waits for them, and re-layouts: 2.85 us -> none
    pallas_call x0 -> x1, Pallas kernels: none -> 1.94 us  [shards(): pl.pallas_call(unpack, name='unpack', out_shape=(jax.ShapeDtypeStruct((32...]
where the time goes in v2:
time: 124 us
  Pallas kernels  123 us (99%)
    pallas_call x1, Pallas kernels, shards(): pl.pallas_call(kernel, name='mixer', out_shape=(jax.ShapeDtypeStruct((512...  121 us

profile of v2, /device:TPU:1, one launch (start us, length us, event | category | flops | bytes accessed | tf_op | source)
XLA Modules:
  0.0 123.9 jit_solution(15704660445856140896)
XLA Ops:
  0.6 121.3 %mixer.1 = (bf16[512,512]{1,0:T(8,128)(2,1)}, f32[16,512]{1,0:T(8,128)}, f32[56,128]{1,0:T(8,128)}) custom-call(bf16[32,4,4,512]{3,2,1,0:T(4,128)(2,1)} %x_in.1, bf16[32,4,4,512]{3,2,1,0:T(4,128)(2,1)} %c_in.1, bf16[512,512]{1,0:T(8,128)(2,1)} %w_in.1, bf16[4,32,32]{2,1,0:T(8,128)(2,1)} %ff_in.1, bf16[4,64,64]{2,1,0:T(8,128)(2,1)} %mf_in.1, ...), custom_call_target="tpu_custom_call" | custom-call | tf_op jit(solution)/shard_map/mixer/pallas_call | solution.py:504
  122.0 1.9 %unpack.1 = (bf16[32,4,4,512]{3,2,1,0:T(4,128)(2,1)}, f32[16,512]{1,0:T(8,128)}, f32[4,32,32]{2,1,0:T(8,128)}, f32[4,4,64]{2,1,0:T(4,128)}, f32[4,4,128]{2,1,0:T(4,128)}) custom-call(bf16[512,512]{1,0:T(8,128)(2,1)} %get-tuple-element.8.dt_ref, f32[16,512]{1,0:T(8,128)} %get-tuple-element.9.gg_ref, f32[56,128]{1,0:T(8,128)} %get-tuple-element.10.sm_ref), custom_call_target="tpu_custom_call" | custom-call | tf_op jit(solution)/shard_map/unpack/pallas_call | solution.py:519

commit v3 on v2

--- a/solution.py
+++ b/solution.py
@@ -10,7 +10,7 @@
 F32 = jnp.float32
 SCALE = 1.0 / 512.0
 HIGH = lax.Precision.HIGHEST
-SPLIT = 8
+SPLIT = 11
 
 
 def mm(a, b):
@@ -54,7 +54,7 @@
     aj, ajt, loj, dj, xg, fog, mbg, lbg, gfold, gacc,
     ps_g, pr_g, zs_g, zr_g, row_g, ar_g,
     ps_s, pr_s, row_s, zr_s, row_l, zr_l, few_s, ar_s, big_s, ar_l,
-    zss, zrs, pss, prs, ins,
+    zss, zrs, pss, prs, ins, far,
 ):
     g = lax.axis_index("grp")
     s = lax.axis_index("seq")
@@ -91,13 +91,14 @@
         pl.semaphore_signal(bar, inc=1, device_id=p_id(lax.rem(p + d, 32)), device_id_type=MESH)
         return _
 
-    lax.fori_loop(1, 16, greet_z, 0)
+    lax.fori_loop(1, 5, greet_z, 0)
+    lax.fori_loop(12, 16, greet_z, 0)
     lax.fori_loop(1, 32, greet_p, 0)
 
     def block(t, rows):
         return pl.ds(pl.multiple_of(t * rows, rows), rows)
 
-    def z_send(src, dst, rows, k, first=1, last=16):
+    def z_send(src, dst, rows, k, first=1, last=16, stop=None):
         def step(d, _):
             t = around(d * 7)
             pltpu.make_async_remote_copy(
@@ -107,7 +108,7 @@
             ).start()
             return _
 
-        lax.fori_loop(first, last, step, 0)
+        lax.fori_loop(first, last if stop is None else stop, step, 0)
         if last < 16:
             return
         pltpu.make_async_copy(src.at[block(z, rows)], dst.at[block(z, rows)], zrs.at[k]).start()
@@ -146,6 +147,21 @@
         for copy in leaving:
             copy.wait()
 
+    def z_pair(src, dst, k):
+        def step(d, _):
+            for t in (around(d), around(16 - d)):
+                pltpu.make_async_remote_copy(
+                    src_ref=src.at[block(t, 32)], dst_ref=dst.at[block(z, 32)],
+                    send_sem=zss.at[k], recv_sem=zrs.at[k],
+                    device_id=z_id(t), device_id_type=MESH,
+                ).start()
+            return _
+
+        return step
+
+    def pair(k):
+        return slice(k * 256, k * 256 + 256)
+
     def lanes(j):
         return slice(j * 128, j * 128 + 128)
 
@@ -159,8 +175,17 @@
     xtk = tn(xn[...], bk[...]).astype(BF)
     for k in range(4):
         zs_f[k] = xtk[:, lanes(k)]
-    pl.semaphore_wait(bar, 46)
-    for k in range(4):
+    pl.semaphore_wait(bar, 39)
+    pl.semaphore_signal(far.at[0], inc=1, device_id=z_id(around(4)), device_id_type=MESH)
+    pl.semaphore_signal(far.at[1], inc=1, device_id=z_id(around(12)), device_id_type=MESH)
+    for k in range(2):
+        lax.fori_loop(1, 5, z_pair(zs_f.at[k], zr_f.at[k], k), 0)
+    pl.semaphore_wait(far.at[0], 1)
+    pl.semaphore_wait(far.at[1], 1)
+    for k in range(2):
+        lax.fori_loop(5, 8, z_pair(zs_f.at[k], zr_f.at[k], k), 0)
+        z_send(zs_f.at[k], zr_f.at[k], 32, k, 8, 16, 9)
+    for k in range(2, 4):
         z_send(zs_f.at[k], zr_f.at[k], 32, k)
 
     bj[...] = onehot(r == (c & 31) * 16 + (c >> 7) * 4 + ((c >> 5) & 3))
@@ -171,10 +196,10 @@
     gt = jax.nn.sigmoid(tn(w_ref[...], xtj[...]))
     gate[...] = gt
     dmix = (ctj[...].astype(F32) * gt).astype(BF)
-    for j in range(4):
-        zs_d[j] = dmix[:, lanes(j)]
-    for j in range(4):
-        z_send(zs_d.at[j], zr_d.at[j], 32, 4 + j)
+    for k in range(2):
+        zs_d[k] = dmix[:, pair(k)]
+    for k in range(2):
+        z_send(zs_d.at[k], zr_d.at[k], 32, 4 + k)
 
     pm[...] = onehot(c == (r & 15) * 32 + (r >> 4))
     pmt[...] = onehot(r == (c & 15) * 32 + (c >> 4))
@@ -242,18 +267,17 @@
         z_send(zs_m.at[j], zr_m.at[j], 32, 8 + j)
 
     d_relay(0)
-    d_relay(1)
     m_relay(0)
-    d_relay(2)
     m_relay(1)
     m_relay(2)
-    d_relay(3)
+    d_relay(1)
     m_relay(3)
 
-    for j in range(4):
-        got(pr_d.at[j], prs, 8 + j)
-        for yy in range(2):
-            dj[half(j), lanes(yy)] = pr_d[j, half(yy)]
+    for k in range(2):
+        got(pr_d.at[k], prs, 8 + k)
+        for j in range(2):
+            for yy in range(2):
+                dj[half(2 * k + j), lanes(yy)] = pr_d[k, half(yy), lanes(j)]
     mb = mm(ajt[...], dj[...]).astype(BF)
     for j in range(4):
         for yy in range(2):
@@ -269,9 +293,8 @@
     for k in range(4):
         for yy in range(2):
             at = (k * 2 + yy) * 16
-            ps_b[k, half(yy)] = fb[:, at : at + 16, :].reshape(256, 128)
-    for k in range(2):
-        p_send(ps_b.at[k], pr_b.at[k], 16, 12 + k)
+            ps_b[k // 2, half(yy), lanes(k % 2)] = fb[:, at : at + 16, :].reshape(256, 128)
+    p_send(ps_b.at[0], pr_b.at[0], 16, 12)
 
     for k in range(4):
         for yy in range(2):
@@ -304,13 +327,7 @@
     pack = pack + exact(exact(sel_f, jnp.where(same4, gf, 0.0)), fold_c)
     ps_s[...] = pack
     p_send(ps_s, pr_s, 8, 16)
-    for k in range(2, 4):
-        p_send(ps_b.at[k], pr_b.at[k], 16, 12 + k)
-
-    def b_relay(k):
-        got(pr_b.at[k], prs, 12 + k)
-        zs_b[k] = mm(pmt[...], pr_b[k]).astype(BF)
-        z_send(zs_b.at[k], zr_b.at[k], 32, 12 + k)
+    p_send(ps_b.at[1], pr_b.at[1], 16, 13)
 
     def gate_share(j):
         got(zr_m.at[j], zrs, 8 + j)
@@ -325,14 +342,12 @@
         else:
             ps_g[...] = (gacc[...] + share).astype(BF)
 
-    b_relay(0)
-    gate_share(0)
-    gate_share(1)
-    b_relay(1)
-    gate_share(2)
-    gate_share(3)
+    got(pr_b.at[0], prs, 12)
+    zs_b[0] = mm(pmt[...], pr_b[0]).astype(BF)
+    z_send(zs_b.at[0], zr_b.at[0], 32, 12)
+    for j in range(4):
+        gate_share(j)
     p_send(ps_g, pr_g, 16, 17)
-    b_relay(2)
 
     owner = lax.div(p, 2) == z
     side = lax.rem(p, 2)
@@ -367,9 +382,9 @@
     note(zr_s, zrs, 16)
     note_sent(zr_s, 15, zss.at[16])
 
-    got(pr_b.at[3], prs, 15)
-    zs_b[3] = mm(pmt[...], pr_b[3]).astype(BF)
-    z_send(zs_b.at[3], zr_b.at[3], 32, 15, 1, SPLIT)
+    got(pr_b.at[1], prs, 13)
+    zs_b[1] = mm(pmt[...], pr_b[1]).astype(BF)
+    z_send(zs_b.at[1], zr_b.at[1], 32, 13, 1, SPLIT)
     gterm[...] = nt(nt(bj[...], dpt[...]).astype(BF), w_ref[...])
 
     got(pr_g, prs, 17)
@@ -377,7 +392,7 @@
     for t in range(16):
         zs_g[t] = tot[t : t + 1]
     z_send(zs_g, zr_g, 1, 17)
-    z_send(zs_b.at[3], zr_b.at[3], 32, 15, SPLIT, 16)
+    z_send(zs_b.at[1], zr_b.at[1], 32, 13, SPLIT, 16)
 
     got(zr_s, zrs, 16)
     for h in range(4):
@@ -445,11 +460,10 @@
     pltpu.make_async_copy(row_g, ar_g.at[g], prs.at[20]).start()
     note_sent(ar_g, 15, pss.at[20])
 
-    for k in range(3):
-        got(zr_b.at[k], zrs, 12 + k)
-        gterm[...] += nt(bk[:, lanes(k)], zr_b[k])
-    got(zr_b.at[3], zrs, 15)
-    dt_ref[...] = (gterm[...] + nt(bk[:, lanes(3)], zr_b[3])).astype(BF)
+    got(zr_b.at[0], zrs, 12)
+    gterm[...] += nt(bk[:, pair(0)], zr_b[0])
+    got(zr_b.at[1], zrs, 13)
+    dt_ref[...] = (gterm[...] + nt(bk[:, pair(1)], zr_b[1])).astype(BF)
 
     got(ar_g, prs, 20)
     for q in range(16):
@@ -472,7 +486,7 @@
 
 
 def unpack(dt_ref, gg_ref, sm_ref, d_ref, g_ref, f_ref, m_ref, l_ref):
-    d_ref[...] = dt_ref[...].reshape(32, 4, 4, 512)
+    d_ref[...] = dt_ref[...].reshape(d_ref.shape)
     g_ref[...] = gg_ref[...]
     for h in range(4):
         l_ref[h] = sm_ref[h * 4 : h * 4 + 4]
@@ -485,10 +499,13 @@
 def shards(tokens, cotangent, gate_weight, first_factor, middle_factor, last_factor):
     V = pltpu.VMEM
     big = V((4, 512, 128), BF)
+    two = V((2, 512, 256), BF)
     sq = V((512, 512), BF)
     scratch = (
         [V(a.shape, BF) for a in (tokens, cotangent, gate_weight, first_factor, middle_factor, last_factor)]
-        + [big] * 16
+        + [big, big, two, two] * 2
+        + [big] * 4
+        + [two] * 4
         + [sq, sq, sq, V((512, 512), F32), sq, sq, sq, sq, sq, sq, sq, sq, V((512, 512), F32)]
         + [V((1024, 1024), BF)] * 2
         + [V((1024, 256), BF)] * 2
@@ -499,6 +516,7 @@
         + [V((2, 128), F32), V((16, 2, 128), F32), V((4, 128), F32), V((16, 4, 128), F32), V((8, 128), F32), V((32, 8, 128), F32)]
         + [V((16, 128), F32)] * 2
         + [pltpu.SemaphoreType.DMA((n,)) for n in (19, 19, 21, 21, 6)]
+        + [pltpu.SemaphoreType.REGULAR((2,))]
     )
     vm = pl.BlockSpec(memory_space=V)
     dt, gg, sm = pl.pallas_call(

time: 124 us -> 120 us (0.968)
  Pallas kernels: 123 us -> 120 us
    pallas_call x1, Pallas kernels: 121 us -> 118 us  [shards(): pl.pallas_call(kernel, name='mixer', out_shape=(jax.ShapeDtypeStruct((512...]
where the time goes in v3:
time: 120 us
  Pallas kernels  120 us (100%)
    pallas_call x1, Pallas kernels, shards(): pl.pallas_call(kernel, name='mixer', out_shape=(jax.ShapeDtypeStruct((512...  118 us

profile of v3, /device:TPU:1, one launch (start us, length us, event | category | flops | bytes accessed | tf_op | source)
XLA Modules:
  0.0 120.2 jit_solution(4214202942888573551)
XLA Ops:
  0.6 117.6 %mixer.1 = (bf16[512,512]{1,0:T(8,128)(2,1)}, f32[16,512]{1,0:T(8,128)}, f32[56,128]{1,0:T(8,128)}) custom-call(bf16[32,4,4,512]{3,2,1,0:T(4,128)(2,1)} %x_in.1, bf16[32,4,4,512]{3,2,1,0:T(4,128)(2,1)} %c_in.1, bf16[512,512]{1,0:T(8,128)(2,1)} %w_in.1, bf16[4,32,32]{2,1,0:T(8,128)(2,1)} %ff_in.1, bf16[4,64,64]{2,1,0:T(8,128)(2,1)} %mf_in.1, ...), custom_call_target="tpu_custom_call" | custom-call | tf_op jit(solution)/shard_map/mixer/pallas_call | solution.py:522
  118.2 1.9 %unpack.1 = (bf16[32,4,4,512]{3,2,1,0:T(4,128)(2,1)}, f32[16,512]{1,0:T(8,128)}, f32[4,32,32]{2,1,0:T(8,128)}, f32[4,4,64]{2,1,0:T(4,128)}, f32[4,4,128]{2,1,0:T(4,128)}) custom-call(bf16[512,512]{1,0:T(8,128)(2,1)} %get-tuple-element.8.dt_ref, f32[16,512]{1,0:T(8,128)} %get-tuple-element.9.gg_ref, f32[56,128]{1,0:T(8,128)} %get-tuple-element.10.sm_ref), custom_call_target="tpu_custom_call" | custom-call | tf_op jit(solution)/shard_map/unpack/pallas_call | solution.py:537

commit v4 on v3

--- a/solution.py
+++ b/solution.py
@@ -10,7 +10,7 @@
 F32 = jnp.float32
 SCALE = 1.0 / 512.0
 HIGH = lax.Precision.HIGHEST
-SPLIT = 11
+SPLIT = 6
 
 
 def mm(a, b):
@@ -78,8 +78,7 @@
             ((x_in, x_ref), (c_in, c_ref), (w_in, w_ref), (ff_in, ff_ref), (mf_in, mf_ref), (lf_in, lf_ref))
         )
     ]
-    for load in loads:
-        load.start()
+    loads[0].start()
     bar = pltpu.get_barrier_semaphore()
     waiting, leaving = {}, []
 
@@ -171,15 +170,21 @@
     r, c = grid2(512, 512)
     bk[...] = onehot(r == (c & 31) * 16 + ((c >> 5) & 3) * 4 + (c >> 7))
     loads[0].wait()
+    for load in loads[1:]:
+        load.start()
     xn[...] = x_ref[...].reshape(512, 512)
-    xtk = tn(xn[...], bk[...]).astype(BF)
-    for k in range(4):
-        zs_f[k] = xtk[:, lanes(k)]
+    def turn(h):
+        part = tn(xn[...], bk[:, pair(h)]).astype(BF)
+        for k in range(2):
+            zs_f[2 * h + k] = part[:, lanes(k)]
+
+    turn(0)
     pl.semaphore_wait(bar, 39)
     pl.semaphore_signal(far.at[0], inc=1, device_id=z_id(around(4)), device_id_type=MESH)
     pl.semaphore_signal(far.at[1], inc=1, device_id=z_id(around(12)), device_id_type=MESH)
     for k in range(2):
         lax.fori_loop(1, 5, z_pair(zs_f.at[k], zr_f.at[k], k), 0)
+    turn(1)
     pl.semaphore_wait(far.at[0], 1)
     pl.semaphore_wait(far.at[1], 1)
     for k in range(2):

time: 120 us -> 119 us (level)
  Pallas kernels: 120 us -> 118 us
where the time goes in v4:
time: 119 us
  Pallas kernels  118 us (99%)
    pallas_call x1, Pallas kernels, shards(): pl.pallas_call(kernel, name='mixer', out_shape=(jax.ShapeDtypeStruct((512...  116 us

profile of v4, /device:TPU:1, one launch (start us, length us, event | category | flops | bytes accessed | tf_op | source)
XLA Modules:
  0.0 119.0 jit_solution(5954708135325047424)
XLA Ops:
  0.6 116.5 %mixer.1 = (bf16[512,512]{1,0:T(8,128)(2,1)}, f32[16,512]{1,0:T(8,128)}, f32[56,128]{1,0:T(8,128)}) custom-call(bf16[32,4,4,512]{3,2,1,0:T(4,128)(2,1)} %x_in.1, bf16[32,4,4,512]{3,2,1,0:T(4,128)(2,1)} %c_in.1, bf16[512,512]{1,0:T(8,128)(2,1)} %w_in.1, bf16[4,32,32]{2,1,0:T(8,128)(2,1)} %ff_in.1, bf16[4,64,64]{2,1,0:T(8,128)(2,1)} %mf_in.1, ...), custom_call_target="tpu_custom_call" | custom-call | tf_op jit(solution)/shard_map/mixer/pallas_call | solution.py:527
  117.1 1.9 %unpack.1 = (bf16[32,4,4,512]{3,2,1,0:T(4,128)(2,1)}, f32[16,512]{1,0:T(8,128)}, f32[4,32,32]{2,1,0:T(8,128)}, f32[4,4,64]{2,1,0:T(4,128)}, f32[4,4,128]{2,1,0:T(4,128)}) custom-call(bf16[512,512]{1,0:T(8,128)(2,1)} %get-tuple-element.8.dt_ref, f32[16,512]{1,0:T(8,128)} %get-tuple-element.9.gg_ref, f32[56,128]{1,0:T(8,128)} %get-tuple-element.10.sm_ref), custom_call_target="tpu_custom_call" | custom-call | tf_op jit(solution)/shard_map/unpack/pallas_call | solution.py:542
